TPU v7x, 512 devices: a whole 4x4x16 slice. The times are simulated.
512 devices in a mesh: blk: 32 (over x, z_lo), rep: 16 (over z_hi, y, core).
Axes of the slice: x: 4, y: 4, z: 16 (z_hi: 2, z_lo: 8; z = z_hi * 8 + z_lo), core: 2. Of those that a mesh axis runs over, the one named last changes fastest.
Arguments:
- signals: bfloat16 [32768, 8192], P('rep', 'blk'), may hold values from -6 to 6
- omega: float32 [32, 5, 256, 256], P('blk', None, 'rep'), may hold values from -1.2 to 3, as said below
- pattern: int32 [32, 5], P('blk'), may hold values from 0 to 31, as said below
Outputs:
- omega_next: float32 [32, 5, 256, 256], P('blk', None, 'rep')
Inputs may be any that keep to these rules, and one draw needn't show every extreme that they name: pattern[i, 0] = i. For two distinct whole numbers A and B from 1 to 15, the same in every row, pattern[i, 1] to pattern[i, 4] are i + A, i - A, i + B and i - B modulo 32 in some order, the same order in every row. Omega is symmetric: omega[i, k] is the transpose of omega[pattern[i, k], k2] where pattern[pattern[i, k], k2] = i. The diagonal entries of omega[i, 0] lie between 1 and 3.
All inputs are finite; a program needn't handle non-finite values.
Results may differ from a plain program's by a relative error of at most 0.0033.
Values may be sent and summed in bfloat16 or wider, within the bound.
A program may use at most 128 MiB of HBM per device.

v0:
```python
import jax
import jax.numpy as jnp
from jax import lax
from jax.sharding import Mesh
from jax.sharding import PartitionSpec as P

STEP_SIZE = 0.5
PENALTY = 0.1
REP = ("zh", "y", "c")


def fine_mesh(mesh):
    return Mesh(mesh.devices.reshape(4, 8, 2, 4, 2), ("x", "zl", "zh", "y", "c"))


def per_device(signals, omega, pattern):
    x_size = lax.axis_size("x")
    zl_size = lax.axis_size("zl")
    team_count = x_size * zl_size
    replica_count = lax.axis_size(REP)
    team_index = lax.axis_index(("x", "zl"))
    replica_index = lax.axis_index(REP)
    slot_count, tile_rows, width = omega.shape[1:]
    time_length = signals.shape[0] * replica_count
    offsets = jnp.mod(pattern[0] - team_index, team_count)
    own = signals.reshape(zl_size, signals.shape[0] // zl_size, width)
    blocks = lax.all_to_all(own, "zl", 0, 0, tiled=True)
    blocks = lax.all_gather(blocks, "x", axis=0, tiled=True)
    panels = lax.all_gather(omega.astype(jnp.bfloat16), REP, axis=2, tiled=True)
    panels = lax.all_gather(panels, "zl", axis=0, tiled=True)
    rows = lax.axis_index("x") * zl_size + jnp.arange(zl_size, dtype=jnp.int32)
    columns = jnp.mod(rows[:, None] + offsets[None, :], team_count)
    gathered = blocks[columns]
    mixed = jnp.einsum(
        "jktc,jkdc->jtd", gathered, panels, preferred_element_type=jnp.float32
    ).astype(jnp.bfloat16)
    left = jnp.einsum("jtd,jktc->jkdc", mixed, gathered, preferred_element_type=jnp.float32)
    own_terms = lax.psum_scatter(left, REP, scatter_dimension=2, tiled=True)
    own_terms = lax.psum_scatter(own_terms, "zl", scatter_dimension=0, tiled=True)[0]
    flipped = lax.all_to_all(own_terms, REP, 2, 1, tiled=True)
    flipped = jnp.swapaxes(flipped, 1, 2)
    match = offsets[None, :] == jnp.mod(team_count - offsets, team_count)[:, None]
    mirror = jnp.argmax(match, axis=1)
    outgoing = flipped[mirror]
    for level in range(team_count.bit_length() - 1):
        step = 1 << level
        route = [((i + step) % team_count, i) for i in range(team_count)]
        shifted = lax.ppermute(outgoing, ("x", "zl"), route)
        chosen = jnp.mod(offsets // step, 2) == 1
        outgoing = jnp.where(chosen[:, None, None], shifted, outgoing)
    gradient = (own_terms + outgoing) / (2.0 * time_length)
    tiles = omega[0]
    column_ids = jnp.arange(width, dtype=jnp.int32)
    row_ids = replica_index * tile_rows + jnp.arange(tile_rows, dtype=jnp.int32)
    diagonal = column_ids[None, :] == row_ids[:, None]
    diagonal = diagonal[None] & (offsets == 0)[:, None, None]
    gradient = gradient - jnp.where(diagonal, 1.0 / jnp.where(diagonal, tiles, 1.0), 0.0)
    value = tiles - STEP_SIZE * gradient
    shrunk = jnp.sign(value) * jnp.maximum(jnp.abs(value) - STEP_SIZE * PENALTY, 0.0)
    return jnp.where(diagonal, value, shrunk)[None]


def solution(mesh):
    return jax.shard_map(
        per_device,
        mesh=fine_mesh(mesh),
        in_specs=(P(REP, ("x", "zl")), P(("x", "zl"), None, REP, None), P(("x", "zl"), None)),
        out_specs=P(("x", "zl"), None, REP, None),
        check_vma=False,
    )
```

profile of v0, /device:TPU:230, one launch (start us, length us, event | category | flops | bytes accessed | tf_op | source)
XLA Modules:
  0.0 669.5 jit_solution(8638916152552195182)
XLA Ops:
  6.5 55.6 %all_to_all.23 = bf16[8,256,256]{2,1,0:T(8,128)(2,1)} all-to-all(bf16[8,256,256]{2,1,0:T(8,128)(2,1)} %bitcast.50), channel_id=1, replica_groups=mesh['x'=4,'zl'=8,'zh'=2,'y'=4,'c'=2] {'zl'}, dimensions={0} | all-to-all | bytes 2097152 | tf_op jit(solution)/shard_map/all_to_all | solution.py:27
  62.1 0.0 all-gather.3.cloned.1.call-update
  62.1 0.0 all-gather.5.cloned.1.call-start
  62.2 0.9 convert_element_type.6
  63.1 45.3 %all_gather.10 = bf16[1,5,256,256]{3,2,1,0:T(8,128)(2,1)} all-gather(bf16[1,5,16,256]{3,2,1,0:T(8,128)(2,1)S(1)} %convert_element_type.6), channel_id=1, replica_groups=mesh['x'=4,'zl'=8,'zh'=2,'y'=4,'c'=2] {'zh','y','c'}, dimensions={2}, use_global_device_ids=true | all-gather | bytes 696320 | tf_op jit(solution)/shard_map/all_gather | solution.py:29
  108.4 0.0 all-gather.5.cloned.1.call-update
  108.4 0.0 reduce-scatter.3.cloned.1.call-start
  108.5 0.7 fusion.7
  109.2 0.1 compare_select_fusion
  109.2 0.1 reshape.294
  109.3 10.0 %all-gather.3.cloned.1.call-done = bf16[32,256,256]{2,1,0:T(8,128)(2,1)} async-done(((bf16[8,256,256]{2,1,0:T(8,128)(2,1)}), bf16[32,256,256]{2,1,0:T(8,128)(2,1)}) %all-gather.3.cloned.1.call-update) | async-done | bytes 4194320 | tf_op jit(solution)/shard_map/all_gather | solution.py:28
  119.3 6.7 %gather_fusion = bf16[40,256,256]{2,1,0:T(8,128)(2,1)} fusion(bf16[32,256,256]{2,1,0:T(8,128)(2,1)} %all-gather.3.cloned.1.call-done, s32[1024]{0:T(1024)S(1)} %pad_clamp_fusion.1), kind=kCustom, calls=%fused_computation | custom fusion | bytes 10485920 | tf_op jit(solution)/shard_map/gather | solution.py:33
  126.0 114.0 %all-gather.5.cloned.1.call-done = bf16[8,5,256,256]{3,2,1,0:T(8,128)(2,1)} async-done(((bf16[1,5,256,256]{3,2,1,0:T(8,128)(2,1)}), bf16[8,5,256,256]{3,2,1,0:T(8,128)(2,1)}) %all-gather.5.cloned.1.call-update) | async-done | bytes 5242896 | tf_op jit(solution)/shard_map/all_gather | solution.py:30
  240.0 12.5 %convolution_bitcast_fusion = f32[8,5,256,256]{2,3,1,0:T(8,128)} fusion(bf16[8,5,256,256]{3,2,1,0:T(8,128)(2,1)} %bitcast.46, bf16[8,5,256,256]{3,2,1,0:T(8,128)(2,1)} %all-gather.5.cloned.1.call-done), kind=kOutput, calls=%fused_computation.2 | convolution fusion | flops 2684878848 | bytes 20971520 | tf_op jit(solution)/shard_map/jtd,jktc->jkdc/dot_general | solution.py:37
  252.5 11.6 %copy.24 = f32[8,5,256,256]{3,0,1,2:T(8,128)} copy(f32[8,5,256,256]{2,3,1,0:T(8,128)} %convolution_bitcast_fusion) | data formatting | bytes 20971520 | tf_op jit(solution)/shard_map/jtd,jktc->jkdc/transpose | solution.py:37
  264.1 0.0 reduce-scatter.3.cloned.1.call-update
  264.2 0.0 reduce-scatter.5.cloned.1.call-start
  264.2 245.1 %reduce-scatter.3.cloned.1.call-done = f32[8,5,16,256]{3,0,1,2:T(8,128)} async-done(((f32[8,5,256,256]{3,0,1,2:T(8,128)}), f32[8,5,16,256]{3,0,1,2:T(8,128)}) %reduce-scatter.3.cloned.1.call-update) | async-done | bytes 655376 | tf_op jit(solution)/shard_map/reduce_scatter | solution.py:38
  509.3 2.1 copy.25
  511.5 0.0 reduce-scatter.5.cloned.1.call-update
  511.5 0.7 iota_reduce_fusion
  512.2 58.2 %reduce-scatter.5.cloned.1.call-done = f32[1,5,16,256]{3,2,1,0:T(8,128)} async-done(((f32[8,5,16,256]{3,2,1,0:T(8,128)}), f32[1,5,16,256]{3,2,1,0:T(8,128)}) %reduce-scatter.5.cloned.1.call-update) | async-done | bytes 81936 | tf_op jit(solution)/shard_map/reduce_scatter | solution.py:39
  570.4 1.4 copy.26
  571.8 1.0 reshape.312
  572.8 14.2 %all-to-all-start.1 = ((f32[16,1,1280]{2,1,0:T(1,128)}), f32[16,1,1280]{2,1,0:T(1,128)S(1)}, u32[]{:S(2)}, u32[]{:S(2)}) async-start(f32[16,1,1280]{2,1,0:T(1,128)} %reshape.312), calls=%async_computation.3 | async-start | bytes 163840 | tf_op jit(solution)/shard_map/all_to_all | solution.py:40
  587.0 15.0 %all-to-all-done.1 = f32[16,1,1280]{2,1,0:T(1,128)S(1)} async-done(((f32[16,1,1280]{2,1,0:T(1,128)}), f32[16,1,1280]{2,1,0:T(1,128)S(1)}, u32[]{:S(2)}, u32[]{:S(2)}) %all-to-all-start.1) | async-done | bytes 81952 | tf_op jit(solution)/shard_map/all_to_all | solution.py:40
  602.0 0.5 broadcast.611
  602.5 0.8 reduce.19
  603.4 0.3 reshape.313
  603.7 0.4 copy.32
  604.1 0.3 all_to_all.20
  604.4 0.6 gather_fusion.1
  604.9 1.9 collective-permute-start
  606.9 13.1 %collective-permute-done = f32[5,16,256]{2,1,0:T(8,128)S(1)} collective-permute-done((f32[5,16,256]{2,1,0:T(8,128)S(1)}, f32[5,16,256]{2,1,0:T(8,128)S(1)}, u32[]{:S(2)}, u32[]{:S(2)}) %collective-permute-start) | collective-permute-done | bytes 81952 | tf_op jit(solution)/shard_map/ppermute | solution.py:48
  620.0 0.1 broadcast_select_fusion
  620.1 1.9 collective-permute-start.1
  622.0 12.3 %collective-permute-done.1 = f32[5,16,256]{2,1,0:T(8,128)S(1)} collective-permute-done((f32[5,16,256]{2,1,0:T(8,128)S(1)}, f32[5,16,256]{2,1,0:T(8,128)S(1)}, u32[]{:S(2)}, u32[]{:S(2)}) %collective-permute-start.1) | collective-permute-done | bytes 81952 | tf_op jit(solution)/shard_map/ppermute | solution.py:48
  634.2 0.1 broadcast_select_fusion.1
  634.3 1.9 collective-permute-start.2
  636.2 10.4 %collective-permute-done.2 = f32[5,16,256]{2,1,0:T(8,128)S(1)} collective-permute-done((f32[5,16,256]{2,1,0:T(8,128)S(1)}, f32[5,16,256]{2,1,0:T(8,128)S(1)}, u32[]{:S(2)}, u32[]{:S(2)}) %collective-permute-start.2) | collective-permute-done | bytes 81952 | tf_op jit(solution)/shard_map/ppermute | solution.py:48
  646.7 0.1 broadcast_select_fusion.2
  646.7 1.9 collective-permute-start.3
  648.7 5.6 collective-permute-done.3
  654.3 0.1 broadcast_select_fusion.3
  654.3 1.9 collective-permute-start.4
  656.3 0.1 iota_compare_fusion
  656.3 5.8 collective-permute-done.4
  662.2 0.8 fusion.5
  (15 shorter events, 0.1 us)
Async XLA Ops:
  6.5 112.7 %all-gather.3.cloned.1.call-start = ((), (), s32[]{:S(2)}) async-start(), calls=%async_computation.4 | async-start | bytes 5242880 | tf_op jit(solution)/shard_map/all_gather | solution.py:28
  62.1 177.9 %all-gather.5.cloned.1.call-start = ((), (), s32[]{:S(2)}) async-start(), calls=%async_computation.5 | async-start | bytes 5898240 | tf_op jit(solution)/shard_map/all_gather | solution.py:30
  108.4 400.9 %reduce-scatter.3.cloned.1.call-start = ((), (), s32[]{:S(2)}) async-start(), calls=%async_computation.6 | async-start | bytes 11141120 | tf_op jit(solution)/shard_map/reduce_scatter | solution.py:38
  264.1 247.4 %copy-start.2 = (s32[1,5]{1,0:T(1,128)S(1)}, s32[1,5]{1,0:T(1,128)}, u32[]{:S(2)}) copy-start(s32[1,5]{1,0:T(1,128)} %param.5) | copy-start | bytes 64
  264.2 398.0 %copy-start.1 = (f32[1,5,16,256]{3,2,1,0:T(8,128)S(1)}, f32[1,5,16,256]{3,2,1,0:T(8,128)}, u32[]{:S(2)}) copy-start(f32[1,5,16,256]{3,2,1,0:T(8,128)} %param.4) | copy-start | bytes 245764
  264.2 306.2 %reduce-scatter.5.cloned.1.call-start = ((), (), s32[]{:S(2)}) async-start(), calls=%async_computation.7 | async-start | bytes 737280 | tf_op jit(solution)/shard_map/reduce_scatter | solution.py:39
  570.4 91.8 %copy-start = (f32[1,5,16,256]{3,2,1,0:T(8,128)S(1)}, f32[1,5,16,256]{3,2,1,0:T(8,128)}, u32[]{:S(2)}) copy-start(f32[1,5,16,256]{3,2,1,0:T(8,128)} %reduce-scatter.5.cloned.1.call-done) | copy-start | bytes 245764
  572.8 29.2 %all-to-all-start.1 = ((f32[16,1,1280]{2,1,0:T(1,128)}), f32[16,1,1280]{2,1,0:T(1,128)S(1)}, u32[]{:S(2)}, u32[]{:S(2)}) async-start(f32[16,1,1280]{2,1,0:T(1,128)} %reshape.312), calls=%async_computation.3 | async-start | bytes 163840 | tf_op jit(solution)/shard_map/all_to_all | solution.py:40
  604.9 15.0 %collective-permute-start = (f32[5,16,256]{2,1,0:T(8,128)S(1)}, f32[5,16,256]{2,1,0:T(8,128)S(1)}, u32[]{:S(2)}, u32[]{:S(2)}) collective-permute-start(f32[5,16,256]{2,1,0:T(8,128)S(1)} %gather_fusion.1), channel_id=1, source_target_pairs={{16,0},{32,16},{48,32},{64,48},{80,64},{96,80},{112,96},{128,112},... | collective-permute-start | bytes 245768 | tf_op jit(solution)/shard_map/ppermute | solution.py:48
  620.1 14.2 %collective-permute-start.1 = (f32[5,16,256]{2,1,0:T(8,128)S(1)}, f32[5,16,256]{2,1,0:T(8,128)S(1)}, u32[]{:S(2)}, u32[]{:S(2)}) collective-permute-start(f32[5,16,256]{2,1,0:T(8,128)S(1)} %broadcast_select_fusion), channel_id=1, source_target_pairs={{32,0},{48,16},{64,32},{80,48},{96,64},{112,80},{128,96},{144,112}... | collective-permute-start | bytes 245768 | tf_op jit(solution)/shard_map/ppermute | solution.py:48
  634.3 12.3 %collective-permute-start.2 = (f32[5,16,256]{2,1,0:T(8,128)S(1)}, f32[5,16,256]{2,1,0:T(8,128)S(1)}, u32[]{:S(2)}, u32[]{:S(2)}) collective-permute-start(f32[5,16,256]{2,1,0:T(8,128)S(1)} %broadcast_select_fusion.1), channel_id=1, source_target_pairs={{64,0},{80,16},{96,32},{112,48},{128,64},{144,80},{160,96},{176,11... | collective-permute-start | bytes 245768 | tf_op jit(solution)/shard_map/ppermute | solution.py:48
  646.7 7.5 %collective-permute-start.3 = (f32[5,16,256]{2,1,0:T(8,128)S(1)}, f32[5,16,256]{2,1,0:T(8,128)S(1)}, u32[]{:S(2)}, u32[]{:S(2)}) collective-permute-start(f32[5,16,256]{2,1,0:T(8,128)S(1)} %broadcast_select_fusion.2), channel_id=1, source_target_pairs={{128,0},{144,16},{160,32},{176,48},{192,64},{208,80},{224,96},{240... | collective-permute-start | bytes 245768 | tf_op jit(solution)/shard_map/ppermute | solution.py:48
  654.3 7.8 %collective-permute-start.4 = (f32[5,16,256]{2,1,0:T(8,128)S(1)}, f32[5,16,256]{2,1,0:T(8,128)S(1)}, u32[]{:S(2)}, u32[]{:S(2)}) collective-permute-start(f32[5,16,256]{2,1,0:T(8,128)S(1)} %broadcast_select_fusion.3), channel_id=1, source_target_pairs={{256,0},{272,16},{288,32},{304,48},{320,64},{336,80},{352,96},{368... | collective-permute-start | bytes 245768 | tf_op jit(solution)/shard_map/ppermute | solution.py:48
Sparse Core Ops, SparseCore 0:
  62.2 56.9 all-gather.2
  121.4 118.6 all-gather.4
  264.3 245.0 reduce-scatter.2
  512.3 58.1 reduce-scatter.4
where the time goes:
time: 670 us; the launch traced here: 669 us
  waiting for transfers between devices  490 us (73%)
  blocking collectives  101 us (15%)
  local copies, waits for them, and re-layouts  25 us (4%)
  starting transfers between devices  23.9 us (4%)
  between operations  13.3 us (2%)
  matrix products  12.5 us (2%)
    reduce_scatter x1, waiting for transfers between devices, per_device(): own_terms = lax.psum_scatter(left, REP, scatter_dimension=2, tiled=True)  245 us
    all_gather x1, waiting for transfers between devices, per_device(): panels = lax.all_gather(panels, 'zl', axis=0, tiled=True)  114 us
    reduce_scatter x1, waiting for transfers between devices, per_device(): lax.psum_scatter(own_terms, 'zl', scatter_dimension=0, tiled=True)[0]  58.2 us
    all_to_all x1, blocking collectives, per_device(): blocks = lax.all_to_all(own, 'zl', 0, 0, tiled=True)  55.6 us
    ppermute x5, waiting for transfers between devices, per_device(): shifted = lax.ppermute(outgoing, ('x', 'zl'), route)  47.2 us
    all_gather x1, blocking collectives, per_device(): panels = lax.all_gather(omega.astype(jnp.bfloat16), REP, axis=2, tiled=True)  45.3 us
    all_to_all x1, waiting for transfers between devices, per_device(): flipped = lax.all_to_all(own_terms, REP, 2, 1, tiled=True)  15 us
    all_to_all x1, starting transfers between devices, per_device(): flipped = lax.all_to_all(own_terms, REP, 2, 1, tiled=True)  14.2 us
  transfers between devices with their start and end apart: 10, of which 10 were waited for; matrix products, arithmetic and copies ran while one was open for 1% of the time, Pallas kernels for 0%

commit v1 on v0

--- a/solution.py
+++ b/solution.py
@@ -1,3 +1,4 @@
+import functools
 import jax
 import jax.numpy as jnp
 from jax import lax
@@ -7,6 +8,16 @@
 STEP_SIZE = 0.5
 PENALTY = 0.1
 REP = ("zh", "y", "c")
+
+
+def lead_sides(chunk, comm_axis):
+    tmp = jnp.stack([chunk] * lax.axis_size(comm_axis), 0)
+    val = lax.all_to_all(tmp, comm_axis, 0, 0)
+    new = jnp.concatenate(val, 0)
+    return new
+
+
+watch_the_files = functools.partial(lead_sides, comm_axis="zl")
 
 
 def fine_mesh(mesh):
@@ -27,7 +38,7 @@
     blocks = lax.all_to_all(own, "zl", 0, 0, tiled=True)
     blocks = lax.all_gather(blocks, "x", axis=0, tiled=True)
     panels = lax.all_gather(omega.astype(jnp.bfloat16), REP, axis=2, tiled=True)
-    panels = lax.all_gather(panels, "zl", axis=0, tiled=True)
+    panels = watch_the_files(panels)
     rows = lax.axis_index("x") * zl_size + jnp.arange(zl_size, dtype=jnp.int32)
     columns = jnp.mod(rows[:, None] + offsets[None, :], team_count)
     gathered = blocks[columns]

time: 670 us -> 766 us (1.14)
  waiting for transfers between devices: 490 us -> 583 us
  blocking collectives: 101 us -> 54.6 us
  starting transfers between devices: 23.9 us -> 70.2 us
    all_to_all x0 -> x2, waiting for transfers between devices: none -> 165 us  [the longest x1 165 us: lead_sides(): val = lax.all_to_all(tmp, comm_axis, 0, 0)]
    all_gather x1 -> x0, waiting for transfers between devices: 114 us -> none  [per_device(): panels = lax.all_gather(panels, 'zl', axis=0, tiled=True)]
    all_to_all x1 -> x0, blocking collectives: 55.6 us -> none  [per_device(): blocks = lax.all_to_all(own, 'zl', 0, 0, tiled=True)]
    all_to_all x0 -> x2, starting transfers between devices: none -> 46.4 us  [the longest x1 36.5 us: lead_sides(): val = lax.all_to_all(tmp, comm_axis, 0, 0)]
    all_gather x1, waiting for transfers between devices: 9.95 us -> 53 us  [per_device(): blocks = lax.all_gather(blocks, 'x', axis=0, tiled=True)]
    all_gather x1, blocking collectives: 45.3 us -> 54.6 us  [per_device(): panels = lax.all_gather(omega.astype(jnp.bfloat16), REP, axis=2, tiled=True)]
  transfers between devices with their start and end apart: 10 -> 11, of which waited for: 10 -> 10; matrix products, arithmetic and copies ran while one was open for 1% -> 1% of each run, Pallas kernels for 0% -> 0%
where the time goes in v1:
time: 766 us; the launch traced here: 765 us
  waiting for transfers between devices  583 us (76%)
  starting transfers between devices  70.2 us (9%)
  blocking collectives  54.6 us (7%)
  local copies, waits for them, and re-layouts  27.9 us (4%)
  between operations  13.3 us (2%)
  matrix products  12.5 us (2%)
    reduce_scatter x1, waiting for transfers between devices, per_device(): own_terms = lax.psum_scatter(left, REP, scatter_dimension=2, tiled=True)  243 us
    all_to_all x1, waiting for transfers between devices, lead_sides(): val = lax.all_to_all(tmp, comm_axis, 0, 0)  165 us
    reduce_scatter x1, waiting for transfers between devices, per_device(): lax.psum_scatter(own_terms, 'zl', scatter_dimension=0, tiled=True)[0]  58.4 us
    all_gather x1, blocking collectives, per_device(): panels = lax.all_gather(omega.astype(jnp.bfloat16), REP, axis=2, tiled=True)  54.6 us
    all_gather x1, waiting for transfers between devices, per_device(): blocks = lax.all_gather(blocks, 'x', axis=0, tiled=True)  53 us
    ppermute x5, waiting for transfers between devices, per_device(): shifted = lax.ppermute(outgoing, ('x', 'zl'), route)  47.2 us
    all_to_all x1, starting transfers between devices, lead_sides(): val = lax.all_to_all(tmp, comm_axis, 0, 0)  36.5 us
  transfers between devices with their start and end apart: 11, of which 10 were waited for; matrix products, arithmetic and copies ran while one was open for 1% of the time, Pallas kernels for 0%

profile of v1, /device:TPU:230, one launch (start us, length us, event | category | flops | bytes accessed | tf_op | source)
XLA Modules:
  0.0 765.0 jit_solution(1344722893748260345)
XLA Ops:
  6.5 9.9 %all-to-all-start = ((bf16[8,256,256]{2,1,0:T(8,128)(2,1)}), bf16[8,256,256]{2,1,0:T(8,128)(2,1)S(1)}, u32[]{:S(2)}, u32[]{:S(2)}) async-start(bf16[8,256,256]{2,1,0:T(8,128)(2,1)} %bitcast.60), calls=%async_computation | async-start | bytes 2097152 | tf_op jit(solution)/shard_map/all_to_all | solution.py:38
  16.4 0.9 convert_element_type.6
  17.3 54.6 %all_gather.9 = bf16[1,5,256,256]{3,2,1,0:T(8,128)(2,1)S(1)} all-gather(bf16[1,5,16,256]{3,2,1,0:T(8,128)(2,1)S(1)} %convert_element_type.6), channel_id=1, replica_groups=mesh['x'=4,'zl'=8,'zh'=2,'y'=4,'c'=2] {'zh','y','c'}, dimensions={2}, use_global_device_ids=true | all-gather | bytes 696320 | tf_op jit(solution)/shard_map/all_gather | solution.py:40
  72.0 2.9 stack.2
  74.9 36.5 %all-to-all-start.1 = ((bf16[8,1,5,256,256]{4,3,2,1,0:T(8,128)(2,1)}), bf16[8,1,5,256,256]{4,3,2,1,0:T(8,128)(2,1)}, u32[]{:S(2)}, u32[]{:S(2)}) async-start(bf16[8,1,5,256,256]{4,3,2,1,0:T(8,128)(2,1)} %stack.2), calls=%async_computation.1 | async-start | bytes 10485760 | tf_op jit(solution)/shard_map/all_to_all | solution.py:15
  111.4 0.7 all-gather.2.cloned.1.call-update
  112.1 0.0 reduce-scatter.3.cloned.1.call-start
  112.2 0.1 compare_select_fusion
  112.3 0.1 reshape.301
  112.3 53.0 %all-gather.2.cloned.1.call-done = bf16[32,256,256]{2,1,0:T(8,128)(2,1)} async-done(((bf16[8,256,256]{2,1,0:T(8,128)(2,1)}), bf16[32,256,256]{2,1,0:T(8,128)(2,1)}) %all-gather.2.cloned.1.call-update) | async-done | bytes 4194320 | tf_op jit(solution)/shard_map/all_gather | solution.py:39
  165.4 6.7 gather_fusion
  172.1 165.3 %all-to-all-done.1 = bf16[8,1,5,256,256]{4,3,2,1,0:T(8,128)(2,1)} async-done(((bf16[8,1,5,256,256]{4,3,2,1,0:T(8,128)(2,1)}), bf16[8,1,5,256,256]{4,3,2,1,0:T(8,128)(2,1)}, u32[]{:S(2)}, u32[]{:S(2)}) %all-to-all-start.1) | async-done | bytes 5242912 | tf_op jit(solution)/shard_map/all_to_all | solution.py:15
  337.3 12.5 %convolution_bitcast_fusion = f32[8,5,256,256]{2,3,1,0:T(8,128)} fusion(bf16[8,5,256,256]{3,2,1,0:T(8,128)(2,1)} %bitcast.55, bf16[8,1,5,256,256]{4,3,2,1,0:T(8,128)(2,1)} %all-to-all-done.1), kind=kOutput, calls=%fused_computation.4 | convolution fusion | flops 2684878848 | bytes 20971520 | tf_op jit(solution)/shard_map/jtd,jktc->jkdc/dot_general | solution.py:48
  349.8 11.6 %copy.24 = f32[8,5,256,256]{3,0,1,2:T(8,128)} copy(f32[8,5,256,256]{2,3,1,0:T(8,128)} %convolution_bitcast_fusion) | data formatting | bytes 20971520 | tf_op jit(solution)/shard_map/jtd,jktc->jkdc/transpose | solution.py:48
  361.4 0.0 reduce-scatter.3.cloned.1.call-update
  361.4 0.0 copy-start.2
  361.4 0.0 reduce-scatter.5.cloned.1.call-start
  361.5 243.2 %reduce-scatter.3.cloned.1.call-done = f32[8,5,16,256]{3,0,1,2:T(8,128)} async-done(((f32[8,5,256,256]{3,0,1,2:T(8,128)}), f32[8,5,16,256]{3,0,1,2:T(8,128)}) %reduce-scatter.3.cloned.1.call-update) | async-done | bytes 655376 | tf_op jit(solution)/shard_map/reduce_scatter | solution.py:49
  604.6 2.1 copy.25
  606.8 0.0 reduce-scatter.5.cloned.1.call-update
  606.8 0.7 iota_reduce_fusion
  607.5 58.4 %reduce-scatter.5.cloned.1.call-done = f32[1,5,16,256]{3,2,1,0:T(8,128)} async-done(((f32[8,5,16,256]{3,2,1,0:T(8,128)}), f32[1,5,16,256]{3,2,1,0:T(8,128)}) %reduce-scatter.5.cloned.1.call-update) | async-done | bytes 81936 | tf_op jit(solution)/shard_map/reduce_scatter | solution.py:50
  665.9 1.4 copy.26
  667.3 1.0 reshape.319
  668.3 14.2 %all-to-all-start.2 = ((f32[16,1,1280]{2,1,0:T(1,128)}), f32[16,1,1280]{2,1,0:T(1,128)S(1)}, u32[]{:S(2)}, u32[]{:S(2)}) async-start(f32[16,1,1280]{2,1,0:T(1,128)} %reshape.319), calls=%async_computation.4 | async-start | bytes 163840 | tf_op jit(solution)/shard_map/all_to_all | solution.py:51
  682.5 15.0 %all-to-all-done.2 = f32[16,1,1280]{2,1,0:T(1,128)S(1)} async-done(((f32[16,1,1280]{2,1,0:T(1,128)}), f32[16,1,1280]{2,1,0:T(1,128)S(1)}, u32[]{:S(2)}, u32[]{:S(2)}) %all-to-all-start.2) | async-done | bytes 81952 | tf_op jit(solution)/shard_map/all_to_all | solution.py:51
  697.5 0.5 broadcast.614
  698.0 0.8 reduce.19
  698.9 0.3 reshape.320
  699.2 0.4 copy.32
  699.6 0.3 all_to_all.24
  699.9 0.6 gather_fusion.1
  700.5 1.9 collective-permute-start
  702.4 13.1 %collective-permute-done = f32[5,16,256]{2,1,0:T(8,128)S(1)} collective-permute-done((f32[5,16,256]{2,1,0:T(8,128)S(1)}, f32[5,16,256]{2,1,0:T(8,128)S(1)}, u32[]{:S(2)}, u32[]{:S(2)}) %collective-permute-start) | collective-permute-done | bytes 81952 | tf_op jit(solution)/shard_map/ppermute | solution.py:59
  715.5 0.1 broadcast_select_fusion
  715.6 1.9 collective-permute-start.1
  717.5 12.3 %collective-permute-done.1 = f32[5,16,256]{2,1,0:T(8,128)S(1)} collective-permute-done((f32[5,16,256]{2,1,0:T(8,128)S(1)}, f32[5,16,256]{2,1,0:T(8,128)S(1)}, u32[]{:S(2)}, u32[]{:S(2)}) %collective-permute-start.1) | collective-permute-done | bytes 81952 | tf_op jit(solution)/shard_map/ppermute | solution.py:59
  729.8 0.1 broadcast_select_fusion.1
  729.8 1.9 collective-permute-start.2
  731.8 10.4 %collective-permute-done.2 = f32[5,16,256]{2,1,0:T(8,128)S(1)} collective-permute-done((f32[5,16,256]{2,1,0:T(8,128)S(1)}, f32[5,16,256]{2,1,0:T(8,128)S(1)}, u32[]{:S(2)}, u32[]{:S(2)}) %collective-permute-start.2) | collective-permute-done | bytes 81952 | tf_op jit(solution)/shard_map/ppermute | solution.py:59
  742.2 0.1 broadcast_select_fusion.2
  742.2 1.9 collective-permute-start.3
  744.2 5.6 collective-permute-done.3
  749.8 0.1 broadcast_select_fusion.3
  749.9 1.9 collective-permute-start.4
  751.8 0.1 iota_compare_fusion
  751.9 5.8 collective-permute-done.4
  757.7 0.8 fusion.13
  (18 shorter events, 0.1 us)
Async XLA Ops:
  6.5 65.4 %all-to-all-start = ((bf16[8,256,256]{2,1,0:T(8,128)(2,1)}), bf16[8,256,256]{2,1,0:T(8,128)(2,1)S(1)}, u32[]{:S(2)}, u32[]{:S(2)}) async-start(bf16[8,256,256]{2,1,0:T(8,128)(2,1)} %bitcast.60), calls=%async_computation | async-start | bytes 2097152 | tf_op jit(solution)/shard_map/all_to_all | solution.py:38
  72.0 2.9 copy-start
  74.9 37.3 %copy-start.3 = (s32[1,5]{1,0:T(1,128)S(1)}, s32[1,5]{1,0:T(1,128)}, u32[]{:S(2)}) copy-start(s32[1,5]{1,0:T(1,128)} %param.5) | copy-start | bytes 64
  74.9 262.4 %all-to-all-start.1 = ((bf16[8,1,5,256,256]{4,3,2,1,0:T(8,128)(2,1)}), bf16[8,1,5,256,256]{4,3,2,1,0:T(8,128)(2,1)}, u32[]{:S(2)}, u32[]{:S(2)}) async-start(bf16[8,1,5,256,256]{4,3,2,1,0:T(8,128)(2,1)} %stack.2), calls=%async_computation.1 | async-start | bytes 10485760 | tf_op jit(solution)/shard_map/all_to_all | solution.py:15
  111.4 54.0 %all-gather.2.cloned.1.call-start = ((), (), s32[]{:S(2)}) async-start(), calls=%async_computation.5 | async-start | bytes 5242880 | tf_op jit(solution)/shard_map/all_gather | solution.py:39
  112.1 492.6 %reduce-scatter.3.cloned.1.call-start = ((), (), s32[]{:S(2)}) async-start(), calls=%async_computation.6 | async-start | bytes 11141120 | tf_op jit(solution)/shard_map/reduce_scatter | solution.py:49
  361.4 396.3 %copy-start.2 = (f32[1,5,16,256]{3,2,1,0:T(8,128)S(1)}, f32[1,5,16,256]{3,2,1,0:T(8,128)}, u32[]{:S(2)}) copy-start(f32[1,5,16,256]{3,2,1,0:T(8,128)} %param.4) | copy-start | bytes 245764
  361.4 304.5 %reduce-scatter.5.cloned.1.call-start = ((), (), s32[]{:S(2)}) async-start(), calls=%async_computation.7 | async-start | bytes 737280 | tf_op jit(solution)/shard_map/reduce_scatter | solution.py:50
  665.9 91.7 %copy-start.1 = (f32[1,5,16,256]{3,2,1,0:T(8,128)S(1)}, f32[1,5,16,256]{3,2,1,0:T(8,128)}, u32[]{:S(2)}) copy-start(f32[1,5,16,256]{3,2,1,0:T(8,128)} %reduce-scatter.5.cloned.1.call-done) | copy-start | bytes 245764
  668.3 29.2 %all-to-all-start.2 = ((f32[16,1,1280]{2,1,0:T(1,128)}), f32[16,1,1280]{2,1,0:T(1,128)S(1)}, u32[]{:S(2)}, u32[]{:S(2)}) async-start(f32[16,1,1280]{2,1,0:T(1,128)} %reshape.319), calls=%async_computation.4 | async-start | bytes 163840 | tf_op jit(solution)/shard_map/all_to_all | solution.py:51
  700.5 15.0 %collective-permute-start = (f32[5,16,256]{2,1,0:T(8,128)S(1)}, f32[5,16,256]{2,1,0:T(8,128)S(1)}, u32[]{:S(2)}, u32[]{:S(2)}) collective-permute-start(f32[5,16,256]{2,1,0:T(8,128)S(1)} %gather_fusion.1), channel_id=1, source_target_pairs={{16,0},{32,16},{48,32},{64,48},{80,64},{96,80},{112,96},{128,112},... | collective-permute-start | bytes 245768 | tf_op jit(solution)/shard_map/ppermute | solution.py:59
  715.6 14.2 %collective-permute-start.1 = (f32[5,16,256]{2,1,0:T(8,128)S(1)}, f32[5,16,256]{2,1,0:T(8,128)S(1)}, u32[]{:S(2)}, u32[]{:S(2)}) collective-permute-start(f32[5,16,256]{2,1,0:T(8,128)S(1)} %broadcast_select_fusion), channel_id=1, source_target_pairs={{32,0},{48,16},{64,32},{80,48},{96,64},{112,80},{128,96},{144,112}... | collective-permute-start | bytes 245768 | tf_op jit(solution)/shard_map/ppermute | solution.py:59
  729.8 12.3 %collective-permute-start.2 = (f32[5,16,256]{2,1,0:T(8,128)S(1)}, f32[5,16,256]{2,1,0:T(8,128)S(1)}, u32[]{:S(2)}, u32[]{:S(2)}) collective-permute-start(f32[5,16,256]{2,1,0:T(8,128)S(1)} %broadcast_select_fusion.1), channel_id=1, source_target_pairs={{64,0},{80,16},{96,32},{112,48},{128,64},{144,80},{160,96},{176,11... | collective-permute-start | bytes 245768 | tf_op jit(solution)/shard_map/ppermute | solution.py:59
  742.2 7.5 collective-permute-start.3
  749.9 7.8 %collective-permute-start.4 = (f32[5,16,256]{2,1,0:T(8,128)S(1)}, f32[5,16,256]{2,1,0:T(8,128)S(1)}, u32[]{:S(2)}, u32[]{:S(2)}) collective-permute-start(f32[5,16,256]{2,1,0:T(8,128)S(1)} %broadcast_select_fusion.3), channel_id=1, source_target_pairs={{256,0},{272,16},{288,32},{304,48},{320,64},{336,80},{352,96},{368... | collective-permute-start | bytes 245768 | tf_op jit(solution)/shard_map/ppermute | solution.py:59
Sparse Core Ops, SparseCore 0:
  114.3 51.0 all-gather.1
  361.5 243.0 reduce-scatter.2
  607.7 58.2 reduce-scatter.4
